TPU v7x, 32 devices: a whole 2x2x4 slice. The times are simulated.
32 devices in a mesh: replica: 16 (over z, x, core), shard: 2 (over y).
Axes of the slice: x: 2, y: 2, z: 4, core: 2. Of those that a mesh axis runs over, the one named last changes fastest.
Arguments:
- tokens: bfloat16 [16384, 768], P(('replica', 'shard')), may hold values from -6 to 6
- grad_output: bfloat16 [16384, 768], P(('replica', 'shard')), may hold values from -6 to 6
- w_attn: bfloat16 [2, 2304, 768], P(None, None, 'shard'), may hold values from -0.21875 to 0.21875
- w_proj: bfloat16 [2, 768, 768], P(None, None, 'shard'), may hold values from -0.875 to 0.875
- w_fc: bfloat16 [2, 3072, 768], P(None, None, 'shard'), may hold values from -0.21875 to 0.21875
- w_out: bfloat16 [2, 768, 3072], P(None, None, 'shard'), may hold values from -0.109375 to 0.109375
- ln_gain: bfloat16 [2, 2, 768], P(None, None, 'shard'), may hold values from 0.5 to 1.5
- ln_shift: bfloat16 [2, 2, 768], P(None, None, 'shard'), may hold values from -1.75 to 1.75
- biases: bfloat16 [2, 4, 768], P(None, None, 'shard'), may hold values from -1.75 to 1.75
- fc_bias: bfloat16 [2, 1, 3072], P(None, None, 'shard'), may hold values from -1.75 to 1.75
Outputs:
- output: bfloat16 [16384, 768], P(('replica', 'shard'))
- grad_tokens: bfloat16 [16384, 768], P(('replica', 'shard'))
- grad_w_attn: float32 [2, 2304, 768], P(None, None, 'shard')
- grad_w_proj: float32 [2, 768, 768], P(None, None, 'shard')
- grad_w_fc: float32 [2, 3072, 768], P(None, None, 'shard')
- grad_w_out: float32 [2, 768, 3072], P(None, None, 'shard')
- grad_ln_gain: float32 [2, 2, 768], P(None, None, 'shard')
- grad_ln_shift: float32 [2, 2, 768], P(None, None, 'shard')
- grad_biases: float32 [2, 4, 768], P(None, None, 'shard')
- grad_fc_bias: float32 [2, 1, 3072], P(None, None, 'shard')
All inputs are finite; a program needn't handle non-finite values.
Results may differ from a plain program's by a relative error of at most 0.017.
Values may be sent and summed in bfloat16 or wider, within the bound.
No kernel may reach another device: no remote copies, remote signals or barrier semaphores. Data moves between devices by JAX's collectives and lax.ppermute only.
A program may use at most 320 MiB of HBM per device.

v0:
```python
import jax
import jax.numpy as jnp
from jax import lax
from jax.sharding import PartitionSpec as P

HEADS = 12
LEN = 512


norm_eps = 1e-05
gelu_coef = 0.7978845608028654
masked_score = -1e30


def layer_norm(stream, gain, shift):
    center = jnp.mean(stream, axis=-1, keepdims=True)
    offset = stream - center
    spread = jnp.mean(offset * offset, axis=-1, keepdims=True)
    return offset * lax.rsqrt(spread + norm_eps) * gain + shift


def gelu_tanh(pre_act):
    return (
        0.5
        * pre_act
        * (1.0 + jnp.tanh(gelu_coef * (pre_act + 0.044715 * pre_act * pre_act * pre_act)))
    )


def project(acts, weight):
    return lax.dot_general(
        acts, weight, (((1,), (1,)), ((), ())), preferred_element_type=jnp.float32
    )


def back_project(grads, weight):
    return jnp.dot(grads, weight, preferred_element_type=jnp.float32)


def weight_grad(grads, acts):
    return lax.dot_general(
        grads, acts, (((0,), (0,)), ((), ())), preferred_element_type=jnp.float32
    )


def column_sum(grads):
    return jnp.sum(grads.astype(jnp.float32), axis=0)


def split_heads(flat, seq_count):
    return flat.reshape(seq_count, LEN, HEADS, flat.shape[-1] // HEADS)


def masked_scores(queries, keys_in):
    length = queries.shape[0]
    scale_factor = queries.shape[-1] ** (-0.5)
    raw_scores = (
        jnp.einsum("qhd,khd->hqk", queries, keys_in, preferred_element_type=jnp.float32)
        * scale_factor
    )
    row_ids = lax.broadcasted_iota(jnp.int32, (length, length), 0)
    col_ids = lax.broadcasted_iota(jnp.int32, (length, length), 1)
    return jnp.where((col_ids <= row_ids)[None], raw_scores, masked_score)


def attend_one(inputs):
    queries, keys_in, values_in = inputs
    scores = masked_scores(queries, keys_in)
    row_peak = jnp.max(scores, axis=-1, keepdims=True)
    expd_scores = jnp.exp(scores - row_peak)
    row_total = jnp.sum(expd_scores, axis=-1, keepdims=True)
    probs = (expd_scores / row_total).astype(jnp.bfloat16)
    mixed_out = jnp.einsum("hqk,khd->qhd", probs, values_in, preferred_element_type=jnp.float32)
    return (mixed_out.astype(jnp.bfloat16), row_peak + jnp.log(row_total))


def attend_back(inputs):
    queries, keys_in, values_in, log_total, grad_mixed = inputs
    scale_factor = queries.shape[-1] ** (-0.5)
    probs = jnp.exp(masked_scores(queries, keys_in) - log_total)
    grad_probs = jnp.einsum(
        "qhd,khd->hqk", grad_mixed, values_in, preferred_element_type=jnp.float32
    )
    grad_values = jnp.einsum(
        "hqk,qhd->khd", probs.astype(jnp.bfloat16), grad_mixed, preferred_element_type=jnp.float32
    )
    inner_sum = jnp.sum(grad_probs * probs, axis=-1, keepdims=True)
    grad_scores = (probs * (grad_probs - inner_sum)).astype(jnp.bfloat16)
    grad_queries = (
        jnp.einsum("hqk,khd->qhd", grad_scores, keys_in, preferred_element_type=jnp.float32)
        * scale_factor
    )
    grad_keys = (
        jnp.einsum("hqk,qhd->khd", grad_scores, queries, preferred_element_type=jnp.float32)
        * scale_factor
    )
    return (
        grad_queries.astype(jnp.bfloat16),
        grad_keys.astype(jnp.bfloat16),
        grad_values.astype(jnp.bfloat16),
    )


def layer_forward(stream, params):
    w_attn, w_proj, w_fc, w_out, gains, shifts, biases, fc_bias = params
    rows = stream.shape[0]
    model_width = stream.shape[1]
    seq_count = rows // LEN
    normed = layer_norm(stream, gains[0].astype(jnp.float32), shifts[0].astype(jnp.float32)).astype(
        jnp.bfloat16
    )
    joined = project(normed, w_attn)
    queries = (joined[:, :model_width] + biases[0]).astype(jnp.bfloat16)
    keys_in = joined[:, model_width : 2 * model_width].astype(jnp.bfloat16)
    values_in = (joined[:, 2 * model_width :] + biases[1]).astype(jnp.bfloat16)
    mixed_out, log_total = lax.map(
        attend_one,
        (
            split_heads(queries, seq_count),
            split_heads(keys_in, seq_count),
            split_heads(values_in, seq_count),
        ),
    )
    mixed_out = mixed_out.reshape(rows, model_width)
    middle = stream + project(mixed_out, w_proj) + biases[2]
    normed_two = layer_norm(
        middle, gains[1].astype(jnp.float32), shifts[1].astype(jnp.float32)
    ).astype(jnp.bfloat16)
    pre_act = project(normed_two, w_fc) + fc_bias[0]
    hidden = gelu_tanh(pre_act).astype(jnp.bfloat16)
    result = middle + project(hidden, w_out) + biases[3]
    return (
        result,
        (
            normed,
            queries,
            keys_in,
            values_in,
            mixed_out,
            log_total,
            middle,
            normed_two,
            pre_act,
            hidden,
        ),
    )


def layer_backward(stream, grad_top, params):
    w_attn, w_proj, w_fc, w_out, gains, shifts, biases, fc_bias = params
    rows = stream.shape[0]
    seq_count = rows // LEN
    unused_out, saved = layer_forward(stream, params)
    (
        normed,
        queries,
        keys_in,
        values_in,
        mixed_out,
        log_total,
        middle,
        normed_two,
        pre_act,
        hidden,
    ) = saved
    grad_branch = grad_top.astype(jnp.bfloat16)
    grad_out_weight = weight_grad(grad_branch, hidden)
    grad_out_bias = column_sum(grad_branch)
    grad_hidden = back_project(grad_branch, w_out)
    unused_gelu, gelu_pull = jax.vjp(gelu_tanh, pre_act)
    grad_pre = gelu_pull(grad_hidden)[0].astype(jnp.bfloat16)
    grad_fc_weight = weight_grad(grad_pre, normed_two)
    grad_fc_shift = column_sum(grad_pre)
    grad_normed_two = back_project(grad_pre, w_fc)
    unused_norm, norm_pull_two = jax.vjp(
        layer_norm, middle, gains[1].astype(jnp.float32), shifts[1].astype(jnp.float32)
    )
    grad_middle_part, grad_gain_two, grad_shift_two = norm_pull_two(grad_normed_two)
    grad_middle = grad_top + grad_middle_part
    grad_attn = grad_middle.astype(jnp.bfloat16)
    grad_proj_weight = weight_grad(grad_attn, mixed_out)
    grad_proj_bias = column_sum(grad_attn)
    grad_mixed = back_project(grad_attn, w_proj).astype(jnp.bfloat16)
    grad_queries, grad_keys, grad_values = lax.map(
        attend_back,
        (
            split_heads(queries, seq_count),
            split_heads(keys_in, seq_count),
            split_heads(values_in, seq_count),
            log_total,
            split_heads(grad_mixed, seq_count),
        ),
    )
    grad_queries = grad_queries.reshape(queries.shape)
    grad_values = grad_values.reshape(values_in.shape)
    grad_joined = jnp.concatenate(
        [grad_queries, grad_keys.reshape(keys_in.shape), grad_values], axis=1
    )
    grad_attn_weight = weight_grad(grad_joined, normed)
    grad_normed = back_project(grad_joined, w_attn)
    unused_first, norm_pull_one = jax.vjp(
        layer_norm, stream, gains[0].astype(jnp.float32), shifts[0].astype(jnp.float32)
    )
    grad_stream_part, grad_gain_one, grad_shift_one = norm_pull_one(grad_normed)
    grad_stream = grad_middle + grad_stream_part
    gain_grads = jnp.stack([grad_gain_one, grad_gain_two])
    shift_grads = jnp.stack([grad_shift_one, grad_shift_two])
    bias_grads = jnp.stack(
        [column_sum(grad_queries), column_sum(grad_values), grad_proj_bias, grad_out_bias]
    )
    local_grads = (
        grad_attn_weight,
        grad_proj_weight,
        grad_fc_weight,
        grad_out_weight,
        gain_grads,
        shift_grads,
        bias_grads,
        grad_fc_shift[None],
    )
    return (grad_stream, local_grads)


def on_device(tokens, grad_output, w_attn, w_proj, w_fc, w_out, ln_gain, ln_shift, biases, fc_bias):
    layer_count = w_attn.shape[0]
    stream = tokens.astype(jnp.float32)
    layer_inputs = []
    gathered_layers = []
    for layer_index in range(layer_count):
        params = (
            lax.all_gather(w_attn[layer_index], "shard", axis=1, tiled=True),
            lax.all_gather(w_proj[layer_index], "shard", axis=1, tiled=True),
            lax.all_gather(w_fc[layer_index], "shard", axis=1, tiled=True),
            lax.all_gather(w_out[layer_index], "shard", axis=1, tiled=True),
            lax.all_gather(ln_gain[layer_index], "shard", axis=1, tiled=True),
            lax.all_gather(ln_shift[layer_index], "shard", axis=1, tiled=True),
            lax.all_gather(biases[layer_index], "shard", axis=1, tiled=True),
            lax.all_gather(fc_bias[layer_index], "shard", axis=1, tiled=True),
        )
        layer_inputs.append(stream)
        gathered_layers.append(params)
        stream, unused_saved = layer_forward(stream, params)
    output = stream.astype(jnp.bfloat16)
    grad_stream = grad_output.astype(jnp.float32)
    layer_shares = [None] * layer_count
    for layer_index in reversed(range(layer_count)):
        params = (
            lax.all_gather(w_attn[layer_index], "shard", axis=1, tiled=True),
            lax.all_gather(w_proj[layer_index], "shard", axis=1, tiled=True),
            lax.all_gather(w_fc[layer_index], "shard", axis=1, tiled=True),
            lax.all_gather(w_out[layer_index], "shard", axis=1, tiled=True),
            lax.all_gather(ln_gain[layer_index], "shard", axis=1, tiled=True),
            lax.all_gather(ln_shift[layer_index], "shard", axis=1, tiled=True),
            lax.all_gather(biases[layer_index], "shard", axis=1, tiled=True),
            lax.all_gather(fc_bias[layer_index], "shard", axis=1, tiled=True),
        )
        grad_stream, local_grads = layer_backward(layer_inputs[layer_index], grad_stream, params)
        grad_a, grad_b, grad_c, grad_d, grad_e, grad_f, grad_g, grad_h = local_grads
        shares = (
            lax.psum_scatter(
                grad_a.astype(jnp.bfloat16), "shard", scatter_dimension=1, tiled=True
            ).astype(jnp.float32),
            lax.psum_scatter(
                grad_b.astype(jnp.bfloat16), "shard", scatter_dimension=1, tiled=True
            ).astype(jnp.float32),
            lax.psum_scatter(
                grad_c.astype(jnp.bfloat16), "shard", scatter_dimension=1, tiled=True
            ).astype(jnp.float32),
            lax.psum_scatter(
                grad_d.astype(jnp.bfloat16), "shard", scatter_dimension=1, tiled=True
            ).astype(jnp.float32),
            lax.psum_scatter(
                grad_e.astype(jnp.bfloat16), "shard", scatter_dimension=1, tiled=True
            ).astype(jnp.float32),
            lax.psum_scatter(
                grad_f.astype(jnp.bfloat16), "shard", scatter_dimension=1, tiled=True
            ).astype(jnp.float32),
            lax.psum_scatter(
                grad_g.astype(jnp.bfloat16), "shard", scatter_dimension=1, tiled=True
            ).astype(jnp.float32),
            lax.psum_scatter(
                grad_h.astype(jnp.bfloat16), "shard", scatter_dimension=1, tiled=True
            ).astype(jnp.float32),
        )
        share_a, share_b, share_c, share_d, share_e, share_f, share_g, share_h = shares
        shares = lax.psum(
            (share_a, share_b, share_c, share_d, share_e, share_f, share_g, share_h), "replica"
        )
        layer_shares[layer_index] = shares
    stacked = [jnp.stack([item[member] for item in layer_shares]) for member in range(8)]
    return (
        output,
        grad_stream.astype(jnp.bfloat16),
        stacked[0],
        stacked[1],
        stacked[2],
        stacked[3],
        stacked[4],
        stacked[5],
        stacked[6],
        stacked[7],
    )


def solution(mesh):
    return jax.shard_map(
        on_device,
        mesh=mesh,
        in_specs=(
            P(("replica", "shard"), None),
            P(("replica", "shard"), None),
            P(None, None, "shard"),
            P(None, None, "shard"),
            P(None, None, "shard"),
            P(None, None, "shard"),
            P(None, None, "shard"),
            P(None, None, "shard"),
            P(None, None, "shard"),
            P(None, None, "shard"),
        ),
        out_specs=(
            P(("replica", "shard"), None),
            P(("replica", "shard"), None),
            P(None, None, "shard"),
            P(None, None, "shard"),
            P(None, None, "shard"),
            P(None, None, "shard"),
            P(None, None, "shard"),
            P(None, None, "shard"),
            P(None, None, "shard"),
            P(None, None, "shard"),
        ),
        check_vma=False,
    )
```

profile of v0, /device:TPU:0, one launch (start us, length us, event | category | flops | bytes accessed | tf_op | source)
XLA Modules:
  0.0 1517.4 jit_solution(7269002027306676688)
XLA Ops:
  12.7 5.0 fusion.134
  17.8 5.0 fusion.135
  26.2 5.8 all-gather.8
  91.8 62.0 %all-gather.29.cloned.1.call-done = bf16[1,3072,768]{2,1,0:T(8,128)(2,1)} async-done(((bf16[1,3072,384]{2,1,0:T(8,128)(2,1)}), bf16[1,3072,768]{2,1,0:T(8,128)(2,1)}) %all-gather.29.cloned.1.call-update) | async-done | bytes 4718608 | tf_op jit(solution)/shard_map/all_gather | solution.py:233
  153.8 7.1 fusion.38
  160.9 57.6 %all-gather.31.cloned.1.call-done = bf16[1,768,3072]{2,1,0:T(8,128)(2,1)} async-done(((bf16[1,768,1536]{2,1,0:T(8,128)(2,1)}), bf16[1,768,3072]{2,1,0:T(8,128)(2,1)}) %all-gather.31.cloned.1.call-update) | async-done | bytes 4718608 | tf_op jit(solution)/shard_map/all_gather | solution.py:234
  218.5 7.7 fusion.143
  227.6 41.6 %all-gather.33.cloned.1.call-done = bf16[1,2304,768]{2,1,0:T(8,128)(2,1)} async-done(((bf16[1,2304,384]{2,1,0:T(8,128)(2,1)}), bf16[1,2304,768]{2,1,0:T(8,128)(2,1)}) %all-gather.33.cloned.1.call-update) | async-done | bytes 3538960 | tf_op jit(solution)/shard_map/all_gather | solution.py:231
  286.0 7.4 all-gather.35.cloned.1.call-done
  297.5 60.7 %all-gather.37.cloned.1.call-done = bf16[1,3072,768]{2,1,0:T(8,128)(2,1)} async-done(((bf16[1,3072,384]{2,1,0:T(8,128)(2,1)}), bf16[1,3072,768]{2,1,0:T(8,128)(2,1)}) %all-gather.37.cloned.1.call-update) | async-done | bytes 4718608 | tf_op jit(solution)/shard_map/all_gather | solution.py:233
  358.2 18.6 %fusion.30 = f32[512,3072]{1,0:T(8,128)} fusion(bf16[1,3072,768]{2,1,0:T(8,128)(2,1)} %all-gather.37.cloned.1.call-done, f32[512,768]{1,0:T(8,128)S(1)} %get-tuple-element.217, f32[768]{0:T(1024)} %get-tuple-element.144, f32[768]{0:T(1024)S(1)} %get-tuple-element.142, f32[512]{0:T(512)} %fusion.108, f32[512]{0:T(512)S(1)} %broadcast_multiply_fusion), kind=kOutput, calls=%fused_computation.59 | convolution fusion | flops 2417885184 | bytes 12593152 | tf_op jit(solution)/shard_map/dot_general | solution.py:31
  376.8 46.2 %all-gather.39.cloned.1.call-done = bf16[1,768,3072]{2,1,0:T(8,128)(2,1)} async-done(((bf16[1,768,1536]{2,1,0:T(8,128)(2,1)}), bf16[1,768,3072]{2,1,0:T(8,128)(2,1)}) %all-gather.39.cloned.1.call-update) | async-done | bytes 4718608 | tf_op jit(solution)/shard_map/all_gather | solution.py:234
  423.0 10.8 fusion.145
  446.1 9.6 bitcast_reduce_fusion.2
  455.7 9.6 multiply_reduce_fusion.1
  465.3 7.4 multiply_convert_fusion.1
  480.3 5.7 multiply_reduce_fusion.3
  488.4 11.6 fusion.146
  510.4 6.1 convolution_convert_fusion.4
  516.5 5.8 copy.90
  528.5 14.5 multiply_reduce_fusion
  543.0 7.1 multiply_convert_fusion
  562.6 5.8 copy.88
  569.1 7.3 convolution_convert_fusion.2
  576.5 6.6 copy.98
  583.8 7.8 convolution_convert_fusion.3
  591.6 6.7 copy.96
  598.4 8.4 fusion.40
  607.4 8.0 convolution_convert_fusion.1
  617.1 6.2 fusion.126
  648.9 5.5 bitcast_convert_fusion.4
  654.3 40.2 %reduce-scatter.59.cloned.1.call-done = bf16[384,3072]{1,0:T(8,128)(2,1)} async-done(((bf16[768,3072]{1,0:T(8,128)(2,1)}), bf16[384,3072]{1,0:T(8,128)(2,1)}) %reduce-scatter.59.cloned.1.call-update) | async-done | bytes 2359312
  698.7 58.0 %reduce-scatter.57.cloned.1.call-done = bf16[384,3072]{1,0:T(8,128)(2,1)} async-done(((bf16[768,3072]{1,0:T(8,128)(2,1)}), bf16[384,3072]{1,0:T(8,128)(2,1)}) %reduce-scatter.57.cloned.1.call-update) | async-done | bytes 2359312
  761.0 6.7 bitcast_convert_fusion.2
  767.7 51.3 %reduce-scatter.47.cloned.1.call-done = bf16[768,1536]{1,0:T(8,128)(2,1)} async-done(((bf16[768,3072]{1,0:T(8,128)(2,1)}), bf16[768,1536]{1,0:T(8,128)(2,1)}) %reduce-scatter.47.cloned.1.call-update) | async-done | bytes 2359312 | tf_op jit(solution)/shard_map/reduce_scatter | solution.py:269
  823.4 57.8 %reduce-scatter.45.cloned.1.call-done = bf16[768,1536]{1,0:T(8,128)(2,1)} async-done(((bf16[768,3072]{1,0:T(8,128)(2,1)}), bf16[768,1536]{1,0:T(8,128)(2,1)}) %reduce-scatter.45.cloned.1.call-update) | async-done | bytes 2359312 | tf_op jit(solution)/shard_map/reduce_scatter | solution.py:269
  889.1 9.1 add_convert_fusion.1
  899.1 8.4 reduce-scatter.63.cloned.1.call-done
  908.5 12.3 reduce-scatter.61.cloned.1.call-done
  921.8 12.2 reduce-scatter.65.cloned.1.call-done
  935.0 18.7 %reduce-scatter.75.cloned.1.call-done = bf16[1536,1]{1,0:T(8,128)(2,1)} async-done(((bf16[3072,1]{1,0:T(8,128)(2,1)}), bf16[1536,1]{1,0:T(8,128)(2,1)}) %reduce-scatter.75.cloned.1.call-update) | async-done | bytes 3088
  954.9 12.1 reduce-scatter.71.cloned.1.call-done
  968.0 18.8 %reduce-scatter.73.cloned.1.call-done = bf16[1536,1]{1,0:T(8,128)(2,1)} async-done(((bf16[3072,1]{1,0:T(8,128)(2,1)}), bf16[1536,1]{1,0:T(8,128)(2,1)}) %reduce-scatter.73.cloned.1.call-update) | async-done | bytes 3088
  987.9 12.0 reduce-scatter.69.cloned.1.call-done
  1001.0 64.0 %all-reduce = (f32[1,2,384]{2,1,0:T(2,128)S(1)}, f32[1,2,384]{2,1,0:T(2,128)S(1)}, f32[1,2,384]{2,1,0:T(2,128)S(1)}, f32[1,2,384]{2,1,0:T(2,128)S(1)}, f32[1,4,3...) all-reduce(f32[1,2,384]{2,1,0:T(2,128)S(1)} %bitcast_convert_fusion, ...), channel_id=1, replica_groups=mesh['replica'=16,'shard'=2] {'replica'}, use_global_device_ids=true, to_apply=%region_45.46 | all-reduce | flops 9216 | bytes 73728 | tf_op jit(solution)/shard_map/psum | solution.py:286
  1066.8 423.7 %all-reduce.4.cloned.1.call-done = (f32[1,2304,384]{2,1,0:T(8,128)}, f32[1,2304,384]{2,1,0:T(8,128)}, f32[1,768,384]{2,1,0:T(8,128)}, f32[1,768,384]{2,1,0:T(8,1...) async-done(((f32[1,2304,384]{2,1,0:T(8,128)}, f32[1,2304,384]{2,1,0:T(8,128)}, ...) | async-done | bytes 28311568 | tf_op jit(solution)/shard_map/psum | solution.py:286
  1490.5 7.3 pad_maximum_fusion.2
  1500.3 5.2 pad_maximum_fusion
  (407 shorter events, 209.0 us)
Async XLA Ops:
  7.2 58.0 %all-gather.25.cloned.1.call-start = ((), (), s32[]{:S(2)}) async-start(), calls=%async_computation.18 | async-start | bytes 5308416 | tf_op jit(solution)/shard_map/all_gather | solution.py:231
  11.4 77.6 %all-gather.27.cloned.1.call-start = ((), (), s32[]{:S(2)}) async-start(), calls=%async_computation.19 | async-start | bytes 1769472 | tf_op jit(solution)/shard_map/all_gather | solution.py:232
  12.7 141.2 %all-gather.29.cloned.1.call-start = ((), (), s32[]{:S(2)}) async-start(), calls=%async_computation.20 | async-start | bytes 7077888 | tf_op jit(solution)/shard_map/all_gather | solution.py:233
  17.8 200.7 %all-gather.31.cloned.1.call-start = ((), (), s32[]{:S(2)}) async-start(), calls=%async_computation.21 | async-start | bytes 7077888 | tf_op jit(solution)/shard_map/all_gather | solution.py:234
  22.8 246.4 %all-gather.33.cloned.1.call-start = ((), (), s32[]{:S(2)}) async-start(), calls=%async_computation.22 | async-start | bytes 5308416 | tf_op jit(solution)/shard_map/all_gather | solution.py:231
  23.4 270.0 %all-gather.35.cloned.1.call-start = ((), (), s32[]{:S(2)}) async-start(), calls=%async_computation.23 | async-start | bytes 1769472 | tf_op jit(solution)/shard_map/all_gather | solution.py:232
  23.5 13.1 copy-start.67
  23.5 22.9 %copy-start.56 = (bf16[2,4,384]{2,1,0:T(4,128)(2,1)S(1)}, bf16[2,4,384]{2,1,0:T(4,128)(2,1)}, u32[]{:S(2)}) copy-start(bf16[2,4,384]{2,1,0:T(4,128)(2,1)} %param.18) | copy-start | bytes 18436
  23.5 32.6 %copy-start.35 = (bf16[2,1,1536]{2,0,1:T(2,128)(2,1)S(1)}, bf16[2,1,1536]{2,0,1:T(2,128)(2,1)}, u32[]{:S(2)}) copy-start(bf16[2,1,1536]{2,0,1:T(2,128)(2,1)} %param.19) | copy-start | bytes 18436
  24.0 334.2 %all-gather.37.cloned.1.call-start = ((), (), s32[]{:S(2)}) async-start(), calls=%async_computation.24 | async-start | bytes 7077888 | tf_op jit(solution)/shard_map/all_gather | solution.py:233
  24.7 398.2 %all-gather.39.cloned.1.call-start = ((), (), s32[]{:S(2)}) async-start(), calls=%async_computation.25 | async-start | bytes 7077888 | tf_op jit(solution)/shard_map/all_gather | solution.py:234
  25.5 608.6 %reduce-scatter.55.cloned.1.call-start = ((), (), s32[]{:S(2)}) async-start(), calls=%async_computation.29 | async-start | bytes 1769472
  25.8 43.6 %copy-start.33 = (f32[512]{0:T(512)}, f32[512]{0:T(512)S(1)}, u32[]{:S(2)}) copy-start(f32[512]{0:T(512)S(1)} %broadcast_multiply_fusion.3) | copy-start | bytes 6148
  26.2 43.2 %copy-start.36 = (f32[512]{0:T(512)}, f32[512]{0:T(512)S(1)}, u32[]{:S(2)}) copy-start(f32[512]{0:T(512)S(1)} %fusion.105) | copy-start | bytes 6148
  45.7 23.7 %copy-start.61 = (f32[768]{0:T(1024)}, f32[768]{0:T(1024)S(1)}, u32[]{:S(2)}) copy-start(f32[768]{0:T(1024)S(1)} %get-tuple-element.149) | copy-start | bytes 9220
  45.7 108.2 %copy-start.58 = (f32[768]{0:T(1024)}, f32[768]{0:T(1024)S(1)}, u32[]{:S(2)}) copy-start(f32[768]{0:T(1024)S(1)} %get-tuple-element.148) | copy-start | bytes 9220
  46.3 222.9 %copy-start.63 = (f32[768]{0:T(1024)}, f32[768]{0:T(1024)S(1)}, u32[]{:S(2)}) copy-start(f32[768]{0:T(1024)S(1)} %get-tuple-element.145) | copy-start | bytes 9220
  46.3 23.1 %copy-start.31 = (f32[768]{0:T(1024)}, f32[768]{0:T(1024)S(1)}, u32[]{:S(2)}) copy-start(f32[768]{0:T(1024)S(1)} %get-tuple-element.147) | copy-start | bytes 9220
  65.2 153.3 %copy-start.40 = (f32[1,1,3072]{2,0,1:T(1,128)}, f32[1,1,3072]{2,0,1:T(1,128)S(1)}, u32[]{:S(2)}) copy-start(f32[1,1,3072]{2,0,1:T(1,128)S(1)} %add.508) | copy-start | bytes 36868
  91.5 127.0 %copy-start.10 = (f32[512,768]{1,0:T(8,128)}, f32[512,768]{1,0:T(8,128)S(1)}, u32[]{:S(2)}) copy-start(f32[512,768]{1,0:T(8,128)S(1)} %get-tuple-element.211) | copy-start | bytes 4718596
  91.8 69.1 %copy-start.45 = (f32[512]{0:T(512)}, f32[512]{0:T(512)S(1)}, u32[]{:S(2)}) copy-start(f32[512]{0:T(512)S(1)} %fusion.106) | copy-start | bytes 6148
  227.6 46.2 %copy-start.52 = (f32[512]{0:T(512)}, f32[512]{0:T(512)S(1)}, u32[]{:S(2)}) copy-start(f32[512]{0:T(512)S(1)} %fusion.107) | copy-start | bytes 6148
  296.3 137.5 %copy-start.8 = (f32[512,768]{1,0:T(8,128)}, f32[512,768]{1,0:T(8,128)S(1)}, u32[]{:S(2)}) copy-start(f32[512,768]{1,0:T(8,128)S(1)} %get-tuple-element.217) | copy-start | bytes 4718596
  446.1 19.2 %slice-start.3 = ((s8[12582912]{0:T(1024)(128)(4,1)}), s8[4194304]{0:T(1024)(128)(4,1)S(1)}, s32[]{:S(2)}) async-start(s8[12582912]{0:T(1024)(128)(4,1)} %bitcast.220), calls=%async_computation.44 | async-start | bytes 8388608
  446.1 19.2 %slice-start.4 = ((s8[12582912]{0:T(1024)(128)(4,1)}), s8[4194304]{0:T(1024)(128)(4,1)S(1)}, s32[]{:S(2)}) async-start(s8[12582912]{0:T(1024)(128)(4,1)} %bitcast.220), calls=%async_computation.45 | async-start | bytes 8388608
  480.2 156.0 %reduce-scatter.53.cloned.1.call-start = ((), (), s32[]{:S(2)}) async-start(), calls=%async_computation.28 | async-start | bytes 1769472
  487.2 12.8 slice-start.14
  488.4 11.6 copy-start.11
  488.4 11.6 copy-start.46
  488.4 11.6 slice-start.15
  510.1 131.0 %reduce-scatter.51.cloned.1.call-start = ((), (), s32[]{:S(2)}) async-start(), calls=%async_computation.27 | async-start | bytes 5308416
  522.3 122.7 %reduce-scatter.49.cloned.1.call-start = ((), (), s32[]{:S(2)}) async-start(), calls=%async_computation.26 | async-start | bytes 5308416
  528.5 14.5 slice-start
  528.5 14.5 slice-start.1
  528.5 14.5 slice-start.2
  568.5 126.0 %reduce-scatter.59.cloned.1.call-start = ((), (), s32[]{:S(2)}) async-start(), calls=%async_computation.31 | async-start | bytes 7077888
  583.1 173.6 %reduce-scatter.57.cloned.1.call-start = ((), (), s32[]{:S(2)}) async-start(), calls=%async_computation.30 | async-start | bytes 7077888
  598.3 220.6 %reduce-scatter.47.cloned.1.call-start = ((), (), s32[]{:S(2)}) async-start(), calls=%async_computation.17 | async-start | bytes 7077888 | tf_op jit(solution)/shard_map/reduce_scatter | solution.py:269
  606.8 274.5 %reduce-scatter.45.cloned.1.call-start = ((), (), s32[]{:S(2)}) async-start(), calls=%async_computation.16 | async-start | bytes 7077888 | tf_op jit(solution)/shard_map/reduce_scatter | solution.py:269
  615.5 282.6 %reduce-scatter.67.cloned.1.call-start = ((), (), s32[]{:S(2)}) async-start(), calls=%async_computation.35 | async-start | bytes 294912
  623.4 284.1 %reduce-scatter.63.cloned.1.call-start = ((), (), s32[]{:S(2)}) async-start(), calls=%async_computation.33 | async-start | bytes 294912
  626.7 294.1 %reduce-scatter.61.cloned.1.call-start = ((), (), s32[]{:S(2)}) async-start(), calls=%async_computation.32 | async-start | bytes 294912
  627.7 306.3 %reduce-scatter.65.cloned.1.call-start = ((), (), s32[]{:S(2)}) async-start(), calls=%async_computation.34 | async-start | bytes 294912
  628.6 325.1 %reduce-scatter.75.cloned.1.call-start = ((), (), s32[]{:S(2)}) async-start(), calls=%async_computation.39 | async-start | bytes 1179648
  630.3 336.8 %reduce-scatter.71.cloned.1.call-start = ((), (), s32[]{:S(2)}) async-start(), calls=%async_computation.37 | async-start | bytes 294912
  631.2 355.6 %reduce-scatter.73.cloned.1.call-start = ((), (), s32[]{:S(2)}) async-start(), calls=%async_computation.38 | async-start | bytes 1179648
  632.9 367.1 %reduce-scatter.69.cloned.1.call-start = ((), (), s32[]{:S(2)}) async-start(), calls=%async_computation.36 | async-start | bytes 294912
  633.8 856.7 %all-reduce.4.cloned.1.call-start = ((), (), s32[]{:S(2)}) async-start(), calls=%async_computation.40 | async-start | bytes 56623104 | tf_op jit(solution)/shard_map/psum | solution.py:286
  (74 other events, 348.2 us)
Sparse Core Ops, SparseCore 0:
  11.6 52.5 all-gather.24
  66.2 22.7 all-gather.26
  91.2 62.6 all-gather.28
  155.8 62.6 all-gather.30
  219.9 49.3 all-gather.32
  270.6 22.7 all-gather.34
  295.5 62.6 all-gather.36
  360.3 62.6 all-gather.38
  480.3 21.8 reduce-scatter.54
  510.3 21.8 reduce-scatter.52
  534.4 47.7 reduce-scatter.50
  584.3 47.7 reduce-scatter.48
  634.4 60.0 reduce-scatter.58
  696.6 60.0 reduce-scatter.56
  758.9 60.0 reduce-scatter.46
  821.1 60.0 reduce-scatter.44
  883.3 11.0 reduce-scatter.66
  896.5 11.0 reduce-scatter.62
  909.7 11.0 reduce-scatter.60
  922.9 11.0 reduce-scatter.64
  936.2 17.4 reduce-scatter.74
  955.9 11.0 reduce-scatter.70
  969.3 17.4 reduce-scatter.72
  988.9 11.0 reduce-scatter.68
  1006.2 484.2 all-reduce.3
where the time goes:
time: 1530 us; the launch traced here: 1520 us
  waiting for transfers between devices  1010 us (66%)
  matrix products  207 us (14%)
  local copies, waits for them, and re-layouts  102 us (7%)
  blocking collectives  101 us (7%)
  other arithmetic  81.2 us (5%)
  between operations  15.5 us (1%)
    psum x1, waiting for transfers between devices, on_device(): lax.psum((share_a, share_b, share_c, share_d, share_e, share_f, share_g,...  424 us
    unnamed x39, waiting for transfers between devices  195 us
    all_gather x2, waiting for transfers between devices, on_device(): lax.all_gather(w_fc[layer_index], 'shard', axis=1, tiled=True)  123 us
    reduce_scatter x2, waiting for transfers between devices, on_device(): lax.psum_scatter(grad_d.astype(jnp.bfloat16), 'shard', scatter_dimension=...  109 us
    all_gather x2, waiting for transfers between devices, on_device(): lax.all_gather(w_out[layer_index], 'shard', axis=1, tiled=True)  104 us
    unnamed x222, local copies, waits for them, and re-layouts  78 us
    psum x1, blocking collectives, on_device(): lax.psum((share_a, share_b, share_c, share_d, share_e, share_f, share_g,...  64 us
    dot_general x8, matrix products, project(): lax.dot_general(acts, weight, (((1,), (1,)), ((), ())), preferred_element...  56.5 us
  transfers between devices with their start and end apart: 25, of which 19 were waited for; matrix products, arithmetic and copies ran while one was open for 20% of the time, Pallas kernels for 0%

commit v1 on v0

v1 whole, which is shorter than its diff:
```python
import jax
import jax.numpy as jnp
from jax import lax
from jax.experimental import pallas as pl
from jax.experimental.pallas import tpu as pltpu
from jax.sharding import PartitionSpec as P

HEADS = 12
LEN = 512
BLOCK = 256
norm_eps = 1e-05
gelu_coef = 0.7978845608028654
masked_score = -1e30
f32 = jnp.float32
bf16 = jnp.bfloat16


def dot_nt(a, b):
    return lax.dot_general(a, b, (((1,), (1,)), ((), ())), preferred_element_type=f32)


def dot_nn(a, b):
    return lax.dot_general(a, b, (((1,), (0,)), ((), ())), preferred_element_type=f32)


def dot_tn(a, b):
    return lax.dot_general(a, b, (((0,), (0,)), ((), ())), preferred_element_type=f32)


def head_mask(x, j):
    lane = lax.broadcasted_iota(jnp.int32, x.shape, 1)
    keep = (lane < 64) if j == 0 else (lane >= 64)
    return jnp.where(keep, x, jnp.zeros_like(x))


def block_scores(qm, k, at):
    s = dot_nt(qm, k) * 0.125
    rows, cols = s.shape
    row = lax.broadcasted_iota(jnp.int32, (rows, cols), 0) + at
    col = lax.broadcasted_iota(jnp.int32, (rows, cols), 1)
    return jnp.where(col <= row, s, masked_score)


def attn_fwd_kernel(q_ref, k_ref, v_ref, o_ref, lse_ref):
    for i in range(LEN // BLOCK):
        at = i * BLOCK
        top = at + BLOCK
        q = q_ref[at:top, :]
        k = k_ref[:top, :]
        v = v_ref[:top, :]
        out = None
        lses = []
        for j in range(2):
            s = block_scores(head_mask(q, j), k, at)
            peak = jnp.max(s, axis=-1, keepdims=True)
            e = jnp.exp(s - peak)
            total = jnp.sum(e, axis=-1, keepdims=True)
            p = (e * (1.0 / total)).astype(bf16)
            part = dot_nn(p, head_mask(v, j))
            out = part if out is None else out + part
            lses.append(jnp.broadcast_to(peak + jnp.log(total), (BLOCK, 64)))
        o_ref[at:top, :] = out.astype(bf16)
        lse_ref[at:top, :] = jnp.concatenate(lses, axis=1)


def attn_fwd(c):
    pairs = HEADS // 2
    width = c.shape[1] // 3
    seqs = c.shape[0] // LEN
    return pl.pallas_call(
        attn_fwd_kernel,
        grid=(seqs, pairs),
        in_specs=[
            pl.BlockSpec((LEN, 128), lambda t, h: (t, h)),
            pl.BlockSpec((LEN, 128), lambda t, h: (t, h + pairs)),
            pl.BlockSpec((LEN, 128), lambda t, h: (t, h + 2 * pairs)),
        ],
        out_specs=[
            pl.BlockSpec((LEN, 128), lambda t, h: (t, h)),
            pl.BlockSpec((LEN, 128), lambda t, h: (t, h)),
        ],
        out_shape=[
            jax.ShapeDtypeStruct((c.shape[0], width), bf16),
            jax.ShapeDtypeStruct((c.shape[0], width), f32),
        ],
        cost_estimate=pl.CostEstimate(
            flops=12 * LEN * LEN * 64 * 4, bytes_accessed=6 << 20, transcendentals=12 * LEN * LEN
        ),
        name="attn_fwd",
    )(c, c, c)


def attn_bwd_kernel(q_ref, k_ref, v_ref, lse_ref, do_ref, dc_ref, dk_acc, dv_acc):
    h = pl.program_id(1)
    dk_acc[...] = jnp.zeros_like(dk_acc)
    dv_acc[...] = jnp.zeros_like(dv_acc)
    for i in range(LEN // BLOCK):
        at = i * BLOCK
        top = at + BLOCK
        q = q_ref[at:top, :]
        do = do_ref[at:top, :]
        k = k_ref[:top, :]
        v = v_ref[:top, :]
        dq = None
        dk = None
        dv = None
        for j in range(2):
            qm = head_mask(q, j)
            dom = head_mask(do, j)
            s = block_scores(qm, k, at)
            p = jnp.exp(s - lse_ref[at:top, 64 * j : 64 * j + 1])
            dp = dot_nt(dom, v)
            inner = jnp.sum(dp * p, axis=-1, keepdims=True)
            ds = (p * (dp - inner)).astype(bf16)
            dq_j = dot_nn(ds, head_mask(k, j))
            dk_j = dot_tn(ds, qm)
            dv_j = dot_tn(p.astype(bf16), dom)
            dq = dq_j if dq is None else dq + dq_j
            dk = dk_j if dk is None else dk + dk_j
            dv = dv_j if dv is None else dv + dv_j
        dc_ref[at:top, pl.ds(pl.multiple_of(h * 128, 128), 128)] = (dq * 0.125).astype(bf16)
        dk_acc[:top, :] += dk
        dv_acc[:top, :] += dv
    width = dc_ref.shape[1] // 3
    dc_ref[:, pl.ds(pl.multiple_of(width + h * 128, 128), 128)] = (dk_acc[...] * 0.125).astype(bf16)
    dc_ref[:, pl.ds(pl.multiple_of(2 * width + h * 128, 128), 128)] = dv_acc[...].astype(bf16)


def attn_bwd(c, lse, do):
    pairs = HEADS // 2
    seqs = c.shape[0] // LEN
    return pl.pallas_call(
        attn_bwd_kernel,
        grid=(seqs, pairs),
        in_specs=[
            pl.BlockSpec((LEN, 128), lambda t, h: (t, h)),
            pl.BlockSpec((LEN, 128), lambda t, h: (t, h + pairs)),
            pl.BlockSpec((LEN, 128), lambda t, h: (t, h + 2 * pairs)),
            pl.BlockSpec((LEN, 128), lambda t, h: (t, h)),
            pl.BlockSpec((LEN, 128), lambda t, h: (t, h)),
        ],
        out_specs=pl.BlockSpec((LEN, c.shape[1]), lambda t, h: (t, 0)),
        out_shape=jax.ShapeDtypeStruct(c.shape, bf16),
        scratch_shapes=[pltpu.VMEM((LEN, 128), f32), pltpu.VMEM((LEN, 128), f32)],
        cost_estimate=pl.CostEstimate(
            flops=12 * LEN * LEN * 64 * 10, bytes_accessed=8 << 20, transcendentals=12 * LEN * LEN
        ),
        name="attn_bwd",
    )(c, c, c, lse, do)


def wgrad_kernel(at_ref, a_ref, ar_ref, bk_ref, bkr_ref, bs_ref, bsr_ref, keep_ref, send_ref):
    a = a_ref[...]
    ar = ar_ref[...]
    keep_ref[...] = (dot_tn(a, bk_ref[...]) + dot_tn(ar, bkr_ref[...])).astype(bf16)
    send_ref[...] = (dot_tn(a, bs_ref[...]) + dot_tn(ar, bsr_ref[...])).astype(bf16)


def wgrad(at, a, a_in, b, b_in, tn, tc):
    tokens = a.shape[0]
    rows = a.shape[1] // 2
    cols = b.shape[1] // 2
    nt = rows // tn
    ct = cols // tc
    grid_spec = pltpu.PrefetchScalarGridSpec(
        num_scalar_prefetch=1,
        grid=(nt, ct),
        in_specs=[
            pl.BlockSpec((tokens, tn), lambda i, j, s: (0, s[0] * nt + i)),
            pl.BlockSpec((tokens, tn), lambda i, j, s: (0, i)),
            pl.BlockSpec((tokens, tc), lambda i, j, s: (0, s[1] * ct + j)),
            pl.BlockSpec((tokens, tc), lambda i, j, s: (0, s[1] * ct + j)),
            pl.BlockSpec((tokens, tc), lambda i, j, s: (0, (1 - s[1]) * ct + j)),
            pl.BlockSpec((tokens, tc), lambda i, j, s: (0, (1 - s[1]) * ct + j)),
        ],
        out_specs=[
            pl.BlockSpec((tn, tc), lambda i, j, s: (i, j)),
            pl.BlockSpec((tn, tc), lambda i, j, s: (i, j)),
        ],
    )
    return pl.pallas_call(
        wgrad_kernel,
        grid_spec=grid_spec,
        out_shape=[jax.ShapeDtypeStruct((rows, cols), bf16)] * 2,
        cost_estimate=pl.CostEstimate(
            flops=8 * tokens * rows * cols,
            bytes_accessed=2 * tokens * (2 * rows + 4 * cols) + 4 * rows * cols,
            transcendentals=0,
        ),
        name="wgrad",
    )(at, a, a_in, b, b_in, b, b_in)


def layer_norm(stream, gain, shift):
    center = jnp.mean(stream, axis=-1, keepdims=True)
    offset = stream - center
    spread = jnp.mean(offset * offset, axis=-1, keepdims=True)
    scale = lax.rsqrt(spread + norm_eps)
    return (offset * scale * gain + shift).astype(bf16), center, scale


def layer_norm_back(stream, center, scale, gain, u):
    x = (stream - center) * scale
    gu = gain * u
    back = scale * (gu - jnp.mean(gu, axis=-1, keepdims=True) - x * jnp.mean(gu * x, axis=-1, keepdims=True))
    return back, jnp.sum(u * x, axis=0), jnp.sum(u, axis=0)


def gelu_tanh(pre):
    return 0.5 * pre * (1.0 + jnp.tanh(gelu_coef * (pre + 0.044715 * pre * pre * pre)))


def gelu_slope(pre):
    t = jnp.tanh(gelu_coef * (pre + 0.044715 * pre * pre * pre))
    return 0.5 * (1.0 + t) + 0.5 * pre * (1.0 - t * t) * gelu_coef * (1.0 + 3.0 * 0.044715 * pre * pre)


def column_sum(x):
    return jnp.sum(x.astype(f32), axis=0)


def solution(mesh):
    replicas = mesh.shape["replica"]
    levels = replicas.bit_length() - 1
    assert replicas == 1 << levels and levels >= 2

    def flip(x, bit):
        return lax.ppermute(x, "replica", [(i, i ^ (1 << bit)) for i in range(replicas)])

    def across(x):
        return lax.ppermute(x, "shard", [(0, 1), (1, 0)])

    def on_device(tokens, grad_output, w_attn, w_proj, w_fc, w_out, ln_gain, ln_shift, biases, fc_bias):
        place = lax.axis_index("replica")
        side = lax.axis_index("shard")
        bits = [(place >> b) & 1 for b in range(levels)]
        core = bits[0]
        layers = w_attn.shape[0]
        half_d = w_attn.shape[2]
        width = 2 * half_d
        at = jnp.stack([core, side]).astype(jnp.int32)

        def gather(w):
            rows, cols = w.shape
            quarter = rows // 4
            own = core * 2 + bits[1]
            q00 = across(lax.dynamic_slice_in_dim(w, own * quarter, quarter, 0))
            q01 = flip(q00, 1)
            q10 = flip(q00, 0)
            q11 = flip(q01, 0)
            full = jnp.zeros((rows, 2 * cols), bf16)
            full = lax.dynamic_update_slice(full, w, (0, side * cols))
            for piece, where in (
                (q00, own),
                (q01, core * 2 + 1 - bits[1]),
                (q10, (1 - core) * 2 + bits[1]),
                (q11, (1 - core) * 2 + 1 - bits[1]),
            ):
                full = lax.dynamic_update_slice(full, piece, (where * quarter, (1 - side) * cols))
            return full

        small = jnp.concatenate(
            [
                ln_gain.reshape(-1, half_d),
                ln_shift.reshape(-1, half_d),
                biases.reshape(-1, half_d),
                fc_bias.reshape(-1, half_d),
            ]
        )
        small_in = across(small)
        low = jnp.where(side == 0, small, small_in)
        high = jnp.where(side == 0, small_in, small)
        norm_rows = 2 * layers

        def take(start, count):
            return jnp.concatenate([low[start : start + count], high[start : start + count]], axis=1)

        gains = take(0, norm_rows).reshape(layers, 2, width).astype(f32)
        shifts = take(norm_rows, norm_rows).reshape(layers, 2, width).astype(f32)
        bias = take(2 * norm_rows, 4 * layers).reshape(layers, 4, width).astype(f32)
        ff_half = fc_bias.shape[2]
        ff_rows = ff_half // half_d
        ff_at = 2 * norm_rows + 4 * layers
        ff_bias = jnp.concatenate(
            [
                low[ff_at : ff_at + layers * ff_rows].reshape(layers, ff_half),
                high[ff_at : ff_at + layers * ff_rows].reshape(layers, ff_half),
            ],
            axis=1,
        ).astype(f32)

        weights = [[gather(w[n]) for w in (w_attn, w_proj, w_fc, w_out)] for n in range(layers)]

        stream = tokens.astype(f32)
        saved = []
        for n in range(layers):
            wa, wp, wf, wo = weights[n]
            n1, mean1, scale1 = layer_norm(stream, gains[n, 0], shifts[n, 0])
            row = jnp.concatenate([bias[n, 0], jnp.zeros((width,), f32), bias[n, 1]])
            c = (dot_nt(n1, wa) + row).astype(bf16)
            o, lse = attn_fwd(c)
            mid = stream + dot_nt(o, wp) + bias[n, 2]
            n2, mean2, scale2 = layer_norm(mid, gains[n, 1], shifts[n, 1])
            pre = dot_nt(n2, wf) + ff_bias[n]
            act = gelu_tanh(pre).astype(bf16)
            out = mid + dot_nt(act, wo) + bias[n, 3]
            swapped = [flip(x, 0) for x in (n1, o, n2, act)]
            saved.append((stream, n1, mean1, scale1, c, o, lse, mid, n2, mean2, scale2, pre, act, swapped))
            stream = out
        output = stream.astype(bf16)

        def swap_half(x):
            half = x.shape[1] // 2
            return flip(lax.dynamic_slice_in_dim(x, (1 - core) * half, half, 1), 0)

        def reduce_all(keep, send):
            sums = keep.astype(f32) + across(send).astype(f32)
            for b in range(1, levels):
                half = sums.shape[0] // 2
                theirs = lax.dynamic_slice_in_dim(sums, (1 - bits[b]) * half, half, 0).astype(bf16)
                mine = lax.dynamic_slice_in_dim(sums, bits[b] * half, half, 0)
                sums = mine + flip(theirs, b).astype(f32)
            done = sums.astype(bf16)
            for b in reversed(range(levels)):
                other = flip(done, b)
                first = jnp.where(bits[b] == 0, done, other)
                second = jnp.where(bits[b] == 0, other, done)
                done = jnp.concatenate([first, second])
            return done

        def reduce_small(vector):
            mine = jnp.where(side == 0, vector[0], vector[1])
            theirs = jnp.where(side == 0, vector[1], vector[0])
            total = mine + across(theirs)
            for b in range(levels):
                total = total + flip(total, b)
            return total

        grad = grad_output.astype(f32)
        results = [None] * layers
        for n in reversed(range(layers)):
            wa, wp, wf, wo = weights[n]
            stream, n1, mean1, scale1, c, o, lse, mid, n2, mean2, scale2, pre, act, swapped = saved[n]
            n1_in, o_in, n2_in, act_in = swapped
            dm = grad.astype(bf16)
            keep_out = wgrad(at, dm, swap_half(dm), act, act_in, 384, 384)
            dpre = (dot_nn(dm, wo) * gelu_slope(pre)).astype(bf16)
            keep_fc = wgrad(at, dpre, swap_half(dpre), n2, n2_in, 384, 384)
            back2, gain2, shift2 = layer_norm_back(mid, mean2, scale2, gains[n, 1], dot_nn(dpre, wf))
            g1 = grad + back2
            da = g1.astype(bf16)
            keep_proj = wgrad(at, da, swap_half(da), o, o_in, 384, 384)
            do = dot_nn(da, wp).astype(bf16)
            dc = attn_bwd(c, lse, do)
            keep_attn = wgrad(at, dc, swap_half(dc), n1, n1_in, 384, 384)
            back1, gain1, shift1 = layer_norm_back(stream, mean1, scale1, gains[n, 0], dot_nn(dc, wa))
            sum_c = column_sum(dc)
            vectors = [
                gain1,
                gain2,
                shift1,
                shift2,
                sum_c[:width],
                sum_c[2 * width :],
                column_sum(da),
                column_sum(dm),
                column_sum(dpre),
            ]
            grad = g1 + back1
            packed = jnp.concatenate([v.reshape(2, -1) for v in vectors], axis=1)
            tiny = reduce_small(packed)
            results[n] = (
                reduce_all(*keep_attn).astype(f32),
                reduce_all(*keep_proj).astype(f32),
                reduce_all(*keep_fc).astype(f32),
                reduce_all(*keep_out).astype(f32),
                tiny[: 2 * half_d].reshape(2, half_d),
                tiny[2 * half_d : 4 * half_d].reshape(2, half_d),
                tiny[4 * half_d : 8 * half_d].reshape(4, half_d),
                tiny[8 * half_d :].reshape(1, -1),
            )
        stacked = [jnp.stack([results[n][m] for n in range(layers)]) for m in range(8)]
        return (output, grad.astype(bf16), *stacked)

    token_spec = P(("replica", "shard"), None)
    weight_spec = P(None, None, "shard")
    return jax.shard_map(
        on_device,
        mesh=mesh,
        in_specs=(token_spec, token_spec) + (weight_spec,) * 8,
        out_specs=(token_spec, token_spec) + (weight_spec,) * 8,
        check_vma=False,
    )
```

time: 1530 us -> 975 us (0.64)
  waiting for transfers between devices: 1010 us -> 377 us
  local copies, waits for them, and re-layouts: 102 us -> 227 us
  matrix products: 207 us -> 89.2 us
  starting transfers between devices: 1.99 us -> 112 us
  blocking collectives: 101 us -> 0 us
  Pallas kernels: 0 us -> 99.6 us
  other arithmetic: 81.2 us -> 54.1 us
    psum x1 -> x0, waiting for transfers between devices: 424 us -> none  [on_device(): lax.psum((share_a, share_b, share_c, share_d, share_e, share_f, share_g,...]
    ppermute x0 -> x123, waiting for transfers between devices: none -> 377 us  [the longest x104 280 us: flip(): lax.ppermute(x, 'replica', [(i, i ^ 1 << bit) for i in range(replicas)])]
    all_gather x8 -> x0, waiting for transfers between devices: 280 us -> none  [the longest x2 123 us: on_device(): lax.all_gather(w_fc[layer_index], 'shard', axis=1, tiled=True)]
    unnamed x39 -> x0, waiting for transfers between devices: 195 us -> none
    dynamic_update_slice x0 -> x40, local copies, waits for them, and re-layouts: none -> 172 us  [the longest x32 162 us: gather(): lax.dynamic_update_slice(full, piece, (where * quarter, (1 - side) * cols))]
    dot_general x36 -> x16, matrix products: 207 us -> 89.2 us  [the longest x8 46.6 us: dot_nn(): lax.dot_general(a, b, (((1,), (0,)), ((), ())), preferred_element_type=f32)]
    ppermute x0 -> x123, starting transfers between devices: none -> 112 us  [the longest x104 68.5 us: flip(): lax.ppermute(x, 'replica', [(i, i ^ 1 << bit) for i in range(replicas)])]
    reduce_scatter x2 -> x0, waiting for transfers between devices: 109 us -> none  [on_device(): lax.psum_scatter(grad_d.astype(jnp.bfloat16), 'shard', scatter_dimension=...]
  transfers between devices with their start and end apart: 25 -> 123, of which waited for: 19 -> 59; matrix products, arithmetic and copies ran while one was open for 20% -> 36% of each run, Pallas kernels for 0% -> 10%
where the time goes in v1:
time: 975 us; the launch traced here: 962 us
  waiting for transfers between devices  377 us (39%)
  local copies, waits for them, and re-layouts  227 us (23%)
  starting transfers between devices  112 us (11%)
  Pallas kernels  99.6 us (10%)
  matrix products  89.2 us (9%)
  other arithmetic  54.1 us (6%)
    ppermute x104, waiting for transfers between devices, flip(): lax.ppermute(x, 'replica', [(i, i ^ 1 << bit) for i in range(replicas)])  280 us
    dynamic_update_slice x32, local copies, waits for them, and re-layouts, gather(): lax.dynamic_update_slice(full, piece, (where * quarter, (1 - side) * cols))  162 us
    ppermute x19, waiting for transfers between devices, across(): return lax.ppermute(x, 'shard', [(0, 1), (1, 0)])  97.7 us
    ppermute x104, starting transfers between devices, flip(): lax.ppermute(x, 'replica', [(i, i ^ 1 << bit) for i in range(replicas)])  68.5 us
    pallas_call x8, Pallas kernels, wgrad(): pl.pallas_call(wgrad_kernel, grid_spec=grid_spec, out_shape=[jax.ShapeDty...  51.8 us
    dot_general x8, matrix products, dot_nn(): lax.dot_general(a, b, (((1,), (0,)), ((), ())), preferred_element_type=f32)  46.6 us
    ppermute x19, starting transfers between devices, across(): return lax.ppermute(x, 'shard', [(0, 1), (1, 0)])  43.2 us
    dot_general x8, matrix products, dot_nt(): lax.dot_general(a, b, (((1,), (1,)), ((), ())), preferred_element_type=f32)  42.6 us
  transfers between devices with their start and end apart: 123, of which 59 were waited for; matrix products, arithmetic and copies ran while one was open for 36% of the time, Pallas kernels for 10%

profile of v1, /device:TPU:0, one launch (start us, length us, event | category | flops | bytes accessed | tf_op | source)
XLA Modules:
  0.0 962.0 jit_solution(2216158696078241789)
XLA Ops:
  67.7 19.3 %collective-permute-done.17 = bf16[576,384]{1,0:T(8,128)(2,1)} collective-permute-done((bf16[576,384]{1,0:T(8,128)(2,1)}, bf16[576,384]{1,0:T(8,128)(2,1)}, u32[]{:S(2)}, u32[]{:S(2)}) %collective-permute-start.17) | collective-permute-done | bytes 442400 | tf_op jit(solution)/shard_map/ppermute | solution.py:231
  91.7 7.9 collective-permute-done.25
  99.6 9.2 collective-permute-done.29
  114.4 23.5 %collective-permute-done.10 = bf16[768,384]{1,0:T(8,128)(2,1)S(1)} collective-permute-done((bf16[768,384]{1,0:T(8,128)(2,1)}, bf16[768,384]{1,0:T(8,128)(2,1)S(1)}, u32[]{:S(2)}, u32[]{:S(2)}) %collective-permute-start.10) | collective-permute-done | bytes 589856 | tf_op jit(solution)/shard_map/ppermute | solution.py:228
  139.6 11.0 %collective-permute-done.26 = bf16[768,384]{1,0:T(8,128)(2,1)} collective-permute-done((bf16[768,384]{1,0:T(8,128)(2,1)}, bf16[768,384]{1,0:T(8,128)(2,1)}, u32[]{:S(2)}, u32[]{:S(2)}) %collective-permute-start.26) | collective-permute-done | bytes 589856 | tf_op jit(solution)/shard_map/ppermute | solution.py:228
  187.4 6.4 dynamic_update_slice.131
  193.8 6.4 dynamic_update_slice.151
  249.3 6.4 dynamic_update_slice.152
  292.0 9.0 attn_fwd.2
  318.2 9.0 multiply_convert_fusion.1
  327.5 6.6 dynamic_update_slice.139
  344.3 9.0 attn_fwd.3
  363.6 8.1 multiply_convert_fusion
  377.8 7.7 convert_reduce_fusion
  385.5 6.5 multiply_reduce_fusion
  395.6 14.8 %attn_bwd.2.a_ref = bf16[512,2304]{1,0:T(8,128)(2,1)} custom-call(bf16[512,2304]{1,0:T(8,128)(2,1)} %fusion.15.q_ref.k_ref.v_ref, bf16[512,2304]{1,0:T(8,128)(2,1)} %fusion.15.q_ref.k_ref.v_ref, bf16[512,2304]{1,0:T(8,128)(2,1)} %fusion.15.q_ref.k_ref.v_ref, f32[512,768]{1,0:T(8,128)} %get-tuple-element.32.lse_ref, ...), custom_call_target="tpu_custom_call" | custom-call | flops 2013265920 | bytes 8388608 | tf_op jit(solution)/shard_map/attn_bwd/pallas_call | solution.py:132
  416.3 9.7 %convert_reduce_fusion.1 = (f32[3072]{0:T(1024)S(1)}, bf16[512,3072]{1,0:T(8,128)(2,1)S(1)}) fusion(f32[512,3072]{1,0:T(8,128)} %get-tuple-element.197, f32[3072]{0:T(1024)S(1)} %bitcast.111, bf16[512,768]{1,0:T(8,128)(2,1)S(1)} %get-tuple-element.87.a_ref, bf16[768,3072]{1,0:T(8,128)(2,1)} %dynamic_update_slice.139), kind=kOutput, calls=%fused_computation.19 | convolution fusion | flops 2450519040 | bytes 14966784 | tf_op jit(solution)/shard_map/dot_general | solution.py:23
  437.4 15.0 %attn_bwd.3.a_ref = bf16[512,2304]{1,0:T(8,128)(2,1)} custom-call(bf16[512,2304]{1,0:T(8,128)(2,1)} %fusion.14.q_ref.k_ref.v_ref, bf16[512,2304]{1,0:T(8,128)(2,1)} %fusion.14.q_ref.k_ref.v_ref, bf16[512,2304]{1,0:T(8,128)(2,1)} %fusion.14.q_ref.k_ref.v_ref, f32[512,768]{1,0:T(8,128)} %get-tuple-element.33.lse_ref, ...), custom_call_target="tpu_custom_call" | custom-call | flops 2013265920 | bytes 8388608 | tf_op jit(solution)/shard_map/attn_bwd/pallas_call | solution.py:132
  464.9 22.5 %collective-permute-start.113 = (f32[4608]{0:T(1024)S(1)}, f32[4608]{0:T(1024)S(1)}, u32[]{:S(2)}, u32[]{:S(2)}) collective-permute-start(f32[4608]{0:T(1024)S(1)} %get-tuple-element.66), channel_id=1, source_target_pairs={{0,1},{1,0},{2,3},{3,2},{4,5},{5,4},{6,7},{7,6},{8,9},{9,8},{10,11... | collective-permute-start | bytes 55304 | tf_op jit(solution)/shard_map/ppermute | solution.py:231
  487.8 7.4 add_convert_fusion
  525.7 6.9 collective-permute-done.55
  557.2 7.2 collective-permute-done.65
  584.6 6.5 wgrad.9
  616.6 7.5 wgrad.12
  624.7 7.4 wgrad.13
  637.3 16.7 %collective-permute-done.45 = bf16[1152,384]{1,0:T(8,128)(2,1)S(1)} collective-permute-done((bf16[1152,384]{1,0:T(8,128)(2,1)}, bf16[1152,384]{1,0:T(8,128)(2,1)S(1)}, u32[]{:S(2)}, u32[]{:S(2)}) %collective-permute-start.45) | collective-permute-done | bytes 884768 | tf_op jit(solution)/shard_map/ppermute | solution.py:231
  658.4 7.2 collective-permute-done.46
  678.8 7.0 collective-permute-done.75
  687.0 22.1 %collective-permute-done.85 = bf16[1536,384]{1,0:T(8,128)(2,1)S(1)} collective-permute-done((bf16[1536,384]{1,0:T(8,128)(2,1)S(1)}, bf16[1536,384]{1,0:T(8,128)(2,1)S(1)}, u32[]{:S(2)}, u32[]{:S(2)}) %collective-permute-start.85) | collective-permute-done | bytes 1179680 | tf_op jit(solution)/shard_map/ppermute | solution.py:231
  717.1 6.9 collective-permute-done.48
  724.0 7.8 collective-permute-done.39
  741.2 8.0 wgrad.14
  752.3 8.1 wgrad.15
  766.5 7.6 collective-permute-done.41
  781.2 7.6 collective-permute-done.78
  788.9 9.1 collective-permute-done.88
  798.0 8.4 collective-permute-done.79
  806.4 9.7 %collective-permute-done.89 = bf16[192,384]{1,0:T(8,128)(2,1)S(1)} collective-permute-done((bf16[192,384]{1,0:T(8,128)(2,1)S(1)}, bf16[192,384]{1,0:T(8,128)(2,1)S(1)}, u32[]{:S(2)}, u32[]{:S(2)}) %collective-permute-start.89) | collective-permute-done | bytes 147488 | tf_op jit(solution)/shard_map/ppermute | solution.py:228
  816.2 8.9 collective-permute-done.80
  825.6 7.6 collective-permute-done.90
  849.8 12.2 %collective-permute-done.91 = bf16[768,384]{1,0:T(8,128)(2,1)S(1)} collective-permute-done((bf16[768,384]{1,0:T(8,128)(2,1)S(1)}, bf16[768,384]{1,0:T(8,128)(2,1)S(1)}, u32[]{:S(2)}, u32[]{:S(2)}) %collective-permute-start.91) | collective-permute-done | bytes 589856 | tf_op jit(solution)/shard_map/ppermute | solution.py:228
  862.4 12.2 %collective-permute-done.96 = bf16[192,1536]{1,0:T(8,128)(2,1)S(1)} collective-permute-done((bf16[192,1536]{1,0:T(8,128)(2,1)S(1)}, bf16[192,1536]{1,0:T(8,128)(2,1)S(1)}, u32[]{:S(2)}, u32[]{:S(2)}) %collective-permute-start.96) | collective-permute-done | bytes 589856 | tf_op jit(solution)/shard_map/ppermute | solution.py:228
  875.5 9.2 collective-permute-done.106
  886.8 7.6 collective-permute-done.107
  897.7 6.6 collective-permute-done.108
  928.4 8.5 collective-permute-done.101
  937.3 11.3 %collective-permute-done.111 = bf16[192,1536]{1,0:T(8,128)(2,1)S(1)} collective-permute-done((bf16[192,1536]{1,0:T(8,128)(2,1)S(1)}, bf16[192,1536]{1,0:T(8,128)(2,1)S(1)}, u32[]{:S(2)}, u32[]{:S(2)}) %collective-permute-start.111) | collective-permute-done | bytes 589856 | tf_op jit(solution)/shard_map/ppermute | solution.py:228
  949.4 7.1 maximum_convert_fusion
  (716 shorter events, 490.6 us)
Async XLA Ops:
  5.2 60.4 %collective-permute-start.1 = (bf16[576,384]{1,0:T(8,128)(2,1)}, bf16[576,384]{1,0:T(8,128)(2,1)}, u32[]{:S(2)}, u32[]{:S(2)}) collective-permute-start(bf16[576,384]{1,0:T(8,128)(2,1)} %dynamic-slice_bitcast_fusion.5), channel_id=1, source_target_pairs={{0,1},{1,0},{2,3},{3,2},{4,5},{5,4},{6,7},{7,6},{8,9},{9,8},{10,11... | collective-permute-start | bytes 1327112 | tf_op jit(solution)/shard_map/ppermute | solution.py:231
  8.3 48.7 %collective-permute-start = (bf16[24,384]{1,0:T(8,128)(2,1)S(1)}, bf16[24,384]{1,0:T(8,128)(2,1)}, u32[]{:S(2)}, u32[]{:S(2)}) collective-permute-start(bf16[24,384]{1,0:T(8,128)(2,1)S(1)} %pad_maximum_fusion.24), channel_id=1, source_target_pairs={{0,1},{1,0},{2,3},{3,2},{4,5},{5,4},{6,7},{7,6},{8,9},{9,8},{10,11... | collective-permute-start | bytes 55304 | tf_op jit(solution)/shard_map/ppermute | solution.py:231
  9.2 46.3 %collective-permute-start.5 = (bf16[192,384]{1,0:T(8,128)(2,1)}, bf16[192,384]{1,0:T(8,128)(2,1)S(1)}, u32[]{:S(2)}, u32[]{:S(2)}) collective-permute-start(bf16[192,384]{1,0:T(8,128)(2,1)} %dynamic-slice_bitcast_fusion.7), channel_id=1, source_target_pairs={{0,1},{1,0},{2,3},{3,2},{4,5},{5,4},{6,7},{7,6},{8,9},{9,8},{10,11... | collective-permute-start | bytes 442376 | tf_op jit(solution)/shard_map/ppermute | solution.py:231
  17.4 73.5 %collective-permute-start.9 = (bf16[768,384]{1,0:T(8,128)(2,1)S(1)}, bf16[768,384]{1,0:T(8,128)(2,1)}, u32[]{:S(2)}, u32[]{:S(2)}) collective-permute-start(bf16[768,384]{1,0:T(8,128)(2,1)S(1)} %dynamic-slice_bitcast_fusion.3), channel_id=1, source_target_pairs={{0,1},{1,0},{2,3},{3,2},{4,5},{5,4},{6,7},{7,6},{8,9},{9,8},{10,11... | collective-permute-start | bytes 1769480 | tf_op jit(solution)/shard_map/ppermute | solution.py:231
  18.2 38.8 %collective-permute-start.21 = (bf16[192,384]{1,0:T(8,128)(2,1)}, bf16[192,384]{1,0:T(8,128)(2,1)}, u32[]{:S(2)}, u32[]{:S(2)}) collective-permute-start(bf16[192,384]{1,0:T(8,128)(2,1)} %dynamic-slice_bitcast_fusion.6), channel_id=1, source_target_pairs={{0,1},{1,0},{2,3},{3,2},{4,5},{5,4},{6,7},{7,6},{8,9},{9,8},{10,11... | collective-permute-start | bytes 442376 | tf_op jit(solution)/shard_map/ppermute | solution.py:231
  61.0 30.0 %collective-permute-start.13 = (bf16[192,1536]{1,0:T(8,128)(2,1)}, bf16[192,1536]{1,0:T(8,128)(2,1)}, u32[]{:S(2)}, u32[]{:S(2)}) collective-permute-start(bf16[192,1536]{1,0:T(8,128)(2,1)} %dynamic-slice_bitcast_fusion.2), channel_id=1, source_target_pairs={{0,1},{1,0},{2,3},{3,2},{4,5},{5,4},{6,7},{7,6},{8,9},{9,8},{10,11... | collective-permute-start | bytes 1769480 | tf_op jit(solution)/shard_map/ppermute | solution.py:231
  65.6 34.0 %collective-permute-start.25 = (bf16[768,384]{1,0:T(8,128)(2,1)S(1)}, bf16[768,384]{1,0:T(8,128)(2,1)}, u32[]{:S(2)}, u32[]{:S(2)}) collective-permute-start(bf16[768,384]{1,0:T(8,128)(2,1)S(1)} %dynamic-slice_bitcast_fusion.1), channel_id=1, source_target_pairs={{0,1},{1,0},{2,3},{3,2},{4,5},{5,4},{6,7},{7,6},{8,9},{9,8},{10,11... | collective-permute-start | bytes 1769480 | tf_op jit(solution)/shard_map/ppermute | solution.py:231
  66.8 42.0 %collective-permute-start.29 = (bf16[192,1536]{1,0:T(8,128)(2,1)S(1)}, bf16[192,1536]{1,0:T(8,128)(2,1)S(1)}, u32[]{:S(2)}, u32[]{:S(2)}) collective-permute-start(bf16[192,1536]{1,0:T(8,128)(2,1)S(1)} %dynamic-slice_bitcast_fusion), channel_id=1, source_target_pairs={{0,1},{1,0},{2,3},{3,2},{4,5},{5,4},{6,7},{7,6},{8,9},{9,8},{10,11... | collective-permute-start | bytes 1769480 | tf_op jit(solution)/shard_map/ppermute | solution.py:231
  108.8 29.1 %collective-permute-start.14 = (bf16[192,1536]{1,0:T(8,128)(2,1)}, bf16[192,1536]{1,0:T(8,128)(2,1)S(1)}, u32[]{:S(2)}, u32[]{:S(2)}) collective-permute-start(bf16[192,1536]{1,0:T(8,128)(2,1)} %collective-permute-done.13), channel_id=1, source_target_pairs={{0,4},{2,6},{4,0},{6,2},{8,12},{10,14},{12,8},{14,10},{16,20},{18,... | collective-permute-start | bytes 1769480 | tf_op jit(solution)/shard_map/ppermute | solution.py:228
  110.3 29.1 %collective-permute-start.15 = (bf16[192,1536]{1,0:T(8,128)(2,1)}, bf16[192,1536]{1,0:T(8,128)(2,1)S(1)}, u32[]{:S(2)}, u32[]{:S(2)}) collective-permute-start(bf16[192,1536]{1,0:T(8,128)(2,1)} %collective-permute-done.13), channel_id=1, source_target_pairs={{0,2},{2,0},{4,6},{6,4},{8,10},{10,8},{12,14},{14,12},{16,18},{18,... | collective-permute-start | bytes 1769480 | tf_op jit(solution)/shard_map/ppermute | solution.py:228
  110.3 27.5 %collective-permute-start.10 = (bf16[768,384]{1,0:T(8,128)(2,1)}, bf16[768,384]{1,0:T(8,128)(2,1)S(1)}, u32[]{:S(2)}, u32[]{:S(2)}) collective-permute-start(bf16[768,384]{1,0:T(8,128)(2,1)} %collective-permute-done.9), channel_id=1, source_target_pairs={{0,4},{2,6},{4,0},{6,2},{8,12},{10,14},{12,8},{14,10},{16,20},{18,... | collective-permute-start | bytes 1769480 | tf_op jit(solution)/shard_map/ppermute | solution.py:228
  111.7 38.9 %collective-permute-start.26 = (bf16[768,384]{1,0:T(8,128)(2,1)}, bf16[768,384]{1,0:T(8,128)(2,1)}, u32[]{:S(2)}, u32[]{:S(2)}) collective-permute-start(bf16[768,384]{1,0:T(8,128)(2,1)} %collective-permute-done.25), channel_id=1, source_target_pairs={{0,4},{2,6},{4,0},{6,2},{8,12},{10,14},{12,8},{14,10},{16,20},{18,... | collective-permute-start | bytes 1769480 | tf_op jit(solution)/shard_map/ppermute | solution.py:228
  114.4 141.3 %collective-permute-start.11 = (bf16[768,384]{1,0:T(8,128)(2,1)}, bf16[768,384]{1,0:T(8,128)(2,1)S(1)}, u32[]{:S(2)}, u32[]{:S(2)}) collective-permute-start(bf16[768,384]{1,0:T(8,128)(2,1)} %collective-permute-done.9), channel_id=1, source_target_pairs={{0,2},{2,0},{4,6},{6,4},{8,10},{10,8},{12,14},{14,12},{16,18},{18,... | collective-permute-start | bytes 1769480 | tf_op jit(solution)/shard_map/ppermute | solution.py:228
  137.9 124.0 %collective-permute-start.27 = (bf16[768,384]{1,0:T(8,128)(2,1)}, bf16[768,384]{1,0:T(8,128)(2,1)S(1)}, u32[]{:S(2)}, u32[]{:S(2)}) collective-permute-start(bf16[768,384]{1,0:T(8,128)(2,1)} %collective-permute-done.25), channel_id=1, source_target_pairs={{0,2},{2,0},{4,6},{6,4},{8,10},{10,8},{12,14},{14,12},{16,18},{18,... | collective-permute-start | bytes 1769480 | tf_op jit(solution)/shard_map/ppermute | solution.py:228
  137.9 130.6 %collective-permute-start.30 = (bf16[192,1536]{1,0:T(8,128)(2,1)S(1)}, bf16[192,1536]{1,0:T(8,128)(2,1)}, u32[]{:S(2)}, u32[]{:S(2)}) collective-permute-start(bf16[192,1536]{1,0:T(8,128)(2,1)S(1)} %collective-permute-done.29), channel_id=1, source_target_pairs={{0,4},{2,6},{4,0},{6,2},{8,12},{10,14},{12,8},{14,10},{16,20},{18,... | collective-permute-start | bytes 1769480 | tf_op jit(solution)/shard_map/ppermute | solution.py:228
  139.4 135.5 %collective-permute-start.31 = (bf16[192,1536]{1,0:T(8,128)(2,1)S(1)}, bf16[192,1536]{1,0:T(8,128)(2,1)S(1)}, u32[]{:S(2)}, u32[]{:S(2)}) collective-permute-start(bf16[192,1536]{1,0:T(8,128)(2,1)S(1)} %collective-permute-done.29), channel_id=1, source_target_pairs={{0,2},{2,0},{4,6},{6,4},{8,10},{10,8},{12,14},{14,12},{16,18},{18,... | collective-permute-start | bytes 1769480 | tf_op jit(solution)/shard_map/ppermute | solution.py:228
  150.6 130.6 %collective-permute-start.4 = (bf16[576,384]{1,0:T(8,128)(2,1)S(1)}, bf16[576,384]{1,0:T(8,128)(2,1)S(1)}, u32[]{:S(2)}, u32[]{:S(2)}) collective-permute-start(bf16[576,384]{1,0:T(8,128)(2,1)S(1)} %collective-permute-done.2), channel_id=1, source_target_pairs={{0,2},{2,0},{4,6},{6,4},{8,10},{10,8},{12,14},{14,12},{16,18},{18,... | collective-permute-start | bytes 1327112 | tf_op jit(solution)/shard_map/ppermute | solution.py:228
  255.7 318.2 %collective-permute-start.34 = (bf16[512,768]{1,0:T(8,128)(2,1)}, bf16[512,768]{1,0:T(8,128)(2,1)}, u32[]{:S(2)}, u32[]{:S(2)}) collective-permute-start(bf16[512,768]{1,0:T(8,128)(2,1)} %fusion.23.bk_ref.bs_ref), channel_id=1, source_target_pairs={{0,2},{2,0},{4,6},{6,4},{8,10},{10,8},{12,14},{14,12},{16,18},{18,... | collective-permute-start | bytes 2359304 | tf_op jit(solution)/shard_map/ppermute | solution.py:228
  261.8 42.1 %collective-permute-start.20 = (bf16[576,384]{1,0:T(8,128)(2,1)}, bf16[576,384]{1,0:T(8,128)(2,1)}, u32[]{:S(2)}, u32[]{:S(2)}) collective-permute-start(bf16[576,384]{1,0:T(8,128)(2,1)} %collective-permute-done.18), channel_id=1, source_target_pairs={{0,2},{2,0},{4,6},{6,4},{8,10},{10,8},{12,14},{14,12},{16,18},{18,... | collective-permute-start | bytes 1327112 | tf_op jit(solution)/shard_map/ppermute | solution.py:228
  268.4 43.2 %collective-permute-start.12 = (bf16[768,384]{1,0:T(8,128)(2,1)S(1)}, bf16[768,384]{1,0:T(8,128)(2,1)}, u32[]{:S(2)}, u32[]{:S(2)}) collective-permute-start(bf16[768,384]{1,0:T(8,128)(2,1)S(1)} %collective-permute-done.10), channel_id=1, source_target_pairs={{0,2},{2,0},{4,6},{6,4},{8,10},{10,8},{12,14},{14,12},{16,18},{18,... | collective-permute-start | bytes 1769480 | tf_op jit(solution)/shard_map/ppermute | solution.py:228
  274.9 52.3 %collective-permute-start.16 = (bf16[192,1536]{1,0:T(8,128)(2,1)S(1)}, bf16[192,1536]{1,0:T(8,128)(2,1)}, u32[]{:S(2)}, u32[]{:S(2)}) collective-permute-start(bf16[192,1536]{1,0:T(8,128)(2,1)S(1)} %collective-permute-done.14), channel_id=1, source_target_pairs={{0,2},{2,0},{4,6},{6,4},{8,10},{10,8},{12,14},{14,12},{16,18},{18,... | collective-permute-start | bytes 1769480 | tf_op jit(solution)/shard_map/ppermute | solution.py:228
  281.2 76.0 %collective-permute-start.28 = (bf16[768,384]{1,0:T(8,128)(2,1)}, bf16[768,384]{1,0:T(8,128)(2,1)}, u32[]{:S(2)}, u32[]{:S(2)}) collective-permute-start(bf16[768,384]{1,0:T(8,128)(2,1)} %collective-permute-done.26), channel_id=1, source_target_pairs={{0,2},{2,0},{4,6},{6,4},{8,10},{10,8},{12,14},{14,12},{16,18},{18,... | collective-permute-start | bytes 1769480 | tf_op jit(solution)/shard_map/ppermute | solution.py:228
  303.9 67.8 %collective-permute-start.32 = (bf16[192,1536]{1,0:T(8,128)(2,1)}, bf16[192,1536]{1,0:T(8,128)(2,1)}, u32[]{:S(2)}, u32[]{:S(2)}) collective-permute-start(bf16[192,1536]{1,0:T(8,128)(2,1)} %collective-permute-done.30), channel_id=1, source_target_pairs={{0,2},{2,0},{4,6},{6,4},{8,10},{10,8},{12,14},{14,12},{16,18},{18,... | collective-permute-start | bytes 1769480 | tf_op jit(solution)/shard_map/ppermute | solution.py:228
  311.6 304.4 %collective-permute-start.74 = (bf16[512,768]{1,0:T(8,128)(2,1)}, bf16[512,768]{1,0:T(8,128)(2,1)}, u32[]{:S(2)}, u32[]{:S(2)}) collective-permute-start(bf16[512,768]{1,0:T(8,128)(2,1)} %add_convert_fusion.3.bk_ref.bs_ref), channel_id=1, source_target_pairs={{0,2},{2,0},{4,6},{6,4},{8,10},{10,8},{12,14},{14,12},{16,18},{18,... | collective-permute-start | bytes 2359304 | tf_op jit(solution)/shard_map/ppermute | solution.py:228
  327.2 189.5 %collective-permute-start.54 = (bf16[512,768]{1,0:T(8,128)(2,1)}, bf16[512,768]{1,0:T(8,128)(2,1)}, u32[]{:S(2)}, u32[]{:S(2)}) collective-permute-start(bf16[512,768]{1,0:T(8,128)(2,1)} %get-tuple-element.30.bk_ref.bs_ref), channel_id=1, source_target_pairs={{0,2},{2,0},{4,6},{6,4},{8,10},{10,8},{12,14},{14,12},{16,18},{18,... | collective-permute-start | bytes 2359304 | tf_op jit(solution)/shard_map/ppermute | solution.py:228
  464.9 33.4 %collective-permute-start.113 = (f32[4608]{0:T(1024)S(1)}, f32[4608]{0:T(1024)S(1)}, u32[]{:S(2)}, u32[]{:S(2)}) collective-permute-start(f32[4608]{0:T(1024)S(1)} %get-tuple-element.66), channel_id=1, source_target_pairs={{0,1},{1,0},{2,3},{3,2},{4,5},{5,4},{6,7},{7,6},{8,9},{9,8},{10,11... | collective-permute-start | bytes 55304 | tf_op jit(solution)/shard_map/ppermute | solution.py:231
  514.4 35.3 %collective-permute-start.64 = (bf16[512,768]{1,0:T(8,128)(2,1)S(1)}, bf16[512,768]{1,0:T(8,128)(2,1)S(1)}, u32[]{:S(2)}, u32[]{:S(2)}) collective-permute-start(bf16[512,768]{1,0:T(8,128)(2,1)S(1)} %copy-done.30), channel_id=1, source_target_pairs={{0,2},{2,0},{4,6},{6,4},{8,10},{10,8},{12,14},{14,12},{16,18},{18,... | collective-permute-start | bytes 2359304 | tf_op jit(solution)/shard_map/ppermute | solution.py:228
  516.7 32.4 %collective-permute-start.63 = (bf16[512,384]{1,0:T(8,128)(2,1)}, bf16[512,384]{1,0:T(8,128)(2,1)}, u32[]{:S(2)}, u32[]{:S(2)}) collective-permute-start(bf16[512,384]{1,0:T(8,128)(2,1)} %constant_dynamic-slice_fusion.4), channel_id=1, source_target_pairs={{0,2},{2,0},{4,6},{6,4},{8,10},{10,8},{12,14},{14,12},{16,18},{18,... | collective-permute-start | bytes 1179656 | tf_op jit(solution)/shard_map/ppermute | solution.py:228
  549.1 25.4 %collective-permute-start.33 = (bf16[512,1152]{1,0:T(8,128)(2,1)}, bf16[512,1152]{1,0:T(8,128)(2,1)}, u32[]{:S(2)}, u32[]{:S(2)}) collective-permute-start(bf16[512,1152]{1,0:T(8,128)(2,1)} %constant_dynamic-slice_fusion.7), channel_id=1, source_target_pairs={{0,2},{2,0},{4,6},{6,4},{8,10},{10,8},{12,14},{14,12},{16,18},{18,... | collective-permute-start | bytes 3538952 | tf_op jit(solution)/shard_map/ppermute | solution.py:228
  549.1 33.8 %collective-permute-start.43 = (bf16[512,1152]{1,0:T(8,128)(2,1)S(1)}, bf16[512,1152]{1,0:T(8,128)(2,1)}, u32[]{:S(2)}, u32[]{:S(2)}) collective-permute-start(bf16[512,1152]{1,0:T(8,128)(2,1)S(1)} %copy-done.35), channel_id=1, source_target_pairs={{0,2},{2,0},{4,6},{6,4},{8,10},{10,8},{12,14},{14,12},{16,18},{18,... | collective-permute-start | bytes 3538952 | tf_op jit(solution)/shard_map/ppermute | solution.py:228
  573.9 50.2 %collective-permute-start.84 = (bf16[512,768]{1,0:T(8,128)(2,1)}, bf16[512,768]{1,0:T(8,128)(2,1)}, u32[]{:S(2)}, u32[]{:S(2)}) collective-permute-start(bf16[512,768]{1,0:T(8,128)(2,1)} %add_convert_fusion.1.bk_ref.bs_ref), channel_id=1, source_target_pairs={{0,2},{2,0},{4,6},{6,4},{8,10},{10,8},{12,14},{14,12},{16,18},{18,... | collective-permute-start | bytes 2359304 | tf_op jit(solution)/shard_map/ppermute | solution.py:228
  582.2 33.8 %collective-permute-start.73 = (bf16[512,1536]{1,0:T(8,128)(2,1)}, bf16[512,1536]{1,0:T(8,128)(2,1)}, u32[]{:S(2)}, u32[]{:S(2)}) collective-permute-start(bf16[512,1536]{1,0:T(8,128)(2,1)} %constant_dynamic-slice_fusion.3), channel_id=1, source_target_pairs={{0,2},{2,0},{4,6},{6,4},{8,10},{10,8},{12,14},{14,12},{16,18},{18,... | collective-permute-start | bytes 4718600 | tf_op jit(solution)/shard_map/ppermute | solution.py:228
  582.4 41.8 %collective-permute-start.83 = (bf16[512,1536]{1,0:T(8,128)(2,1)}, bf16[512,1536]{1,0:T(8,128)(2,1)}, u32[]{:S(2)}, u32[]{:S(2)}) collective-permute-start(bf16[512,1536]{1,0:T(8,128)(2,1)} %constant_dynamic-slice_fusion.2), channel_id=1, source_target_pairs={{0,2},{2,0},{4,6},{6,4},{8,10},{10,8},{12,14},{14,12},{16,18},{18,... | collective-permute-start | bytes 4718600 | tf_op jit(solution)/shard_map/ppermute | solution.py:228
  616.1 133.1 %collective-permute-start.103 = (bf16[512,384]{1,0:T(8,128)(2,1)}, bf16[512,384]{1,0:T(8,128)(2,1)}, u32[]{:S(2)}, u32[]{:S(2)}) collective-permute-start(bf16[512,384]{1,0:T(8,128)(2,1)} %constant_dynamic-slice_fusion), channel_id=1, source_target_pairs={{0,2},{2,0},{4,6},{6,4},{8,10},{10,8},{12,14},{14,12},{16,18},{18,... | collective-permute-start | bytes 1179656 | tf_op jit(solution)/shard_map/ppermute | solution.py:228
  624.1 116.9 %collective-permute-start.94 = (bf16[512,3072]{1,0:T(8,128)(2,1)S(1)}, bf16[512,3072]{1,0:T(8,128)(2,1)}, u32[]{:S(2)}, u32[]{:S(2)}) collective-permute-start(bf16[512,3072]{1,0:T(8,128)(2,1)S(1)} %copy-done.6), channel_id=1, source_target_pairs={{0,2},{2,0},{4,6},{6,4},{8,10},{10,8},{12,14},{14,12},{16,18},{18,... | collective-permute-start | bytes 9437192 | tf_op jit(solution)/shard_map/ppermute | solution.py:228
  624.2 126.9 %collective-permute-start.104 = (bf16[512,3072]{1,0:T(8,128)(2,1)}, bf16[512,3072]{1,0:T(8,128)(2,1)}, u32[]{:S(2)}, u32[]{:S(2)}) collective-permute-start(bf16[512,3072]{1,0:T(8,128)(2,1)} %get-tuple-element.202.bk_ref.bs_ref), channel_id=1, source_target_pairs={{0,2},{2,0},{4,6},{6,4},{8,10},{10,8},{12,14},{14,12},{16,18},{18,... | collective-permute-start | bytes 9437192 | tf_op jit(solution)/shard_map/ppermute | solution.py:228
  657.0 28.8 %collective-permute-start.75 = (bf16[1536,384]{1,0:T(8,128)(2,1)S(1)}, bf16[1536,384]{1,0:T(8,128)(2,1)S(1)}, u32[]{:S(2)}, u32[]{:S(2)}) collective-permute-start(bf16[1536,384]{1,0:T(8,128)(2,1)S(1)} %copy-done.83), channel_id=1, source_target_pairs={{0,1},{1,0},{2,3},{3,2},{4,5},{5,4},{6,7},{7,6},{8,9},{9,8},{10,11... | collective-permute-start | bytes 3538952 | tf_op jit(solution)/shard_map/ppermute | solution.py:231
  677.5 31.7 %collective-permute-start.85 = (bf16[1536,384]{1,0:T(8,128)(2,1)S(1)}, bf16[1536,384]{1,0:T(8,128)(2,1)S(1)}, u32[]{:S(2)}, u32[]{:S(2)}) collective-permute-start(bf16[1536,384]{1,0:T(8,128)(2,1)S(1)} %copy-done.84), channel_id=1, source_target_pairs={{0,1},{1,0},{2,3},{3,2},{4,5},{5,4},{6,7},{7,6},{8,9},{9,8},{10,11... | collective-permute-start | bytes 3538952 | tf_op jit(solution)/shard_map/ppermute | solution.py:231
  685.8 54.2 %collective-permute-start.93 = (bf16[512,384]{1,0:T(8,128)(2,1)S(1)}, bf16[512,384]{1,0:T(8,128)(2,1)S(1)}, u32[]{:S(2)}, u32[]{:S(2)}) collective-permute-start(bf16[512,384]{1,0:T(8,128)(2,1)S(1)} %copy-done.54), channel_id=1, source_target_pairs={{0,2},{2,0},{4,6},{6,4},{8,10},{10,8},{12,14},{14,12},{16,18},{18,... | collective-permute-start | bytes 1179656 | tf_op jit(solution)/shard_map/ppermute | solution.py:228
  751.1 83.2 %collective-permute-start.95 = (bf16[384,1536]{1,0:T(8,128)(2,1)}, bf16[384,1536]{1,0:T(8,128)(2,1)S(1)}, u32[]{:S(2)}, u32[]{:S(2)}) collective-permute-start(bf16[384,1536]{1,0:T(8,128)(2,1)} %get-tuple-element.47), channel_id=1, source_target_pairs={{0,1},{1,0},{2,3},{3,2},{4,5},{5,4},{6,7},{7,6},{8,9},{9,8},{10,11... | collective-permute-start | bytes 3538952 | tf_op jit(solution)/shard_map/ppermute | solution.py:231
  760.4 75.5 %collective-permute-start.105 = (bf16[384,1536]{1,0:T(8,128)(2,1)}, bf16[384,1536]{1,0:T(8,128)(2,1)S(1)}, u32[]{:S(2)}, u32[]{:S(2)}) collective-permute-start(bf16[384,1536]{1,0:T(8,128)(2,1)} %get-tuple-element.49), channel_id=1, source_target_pairs={{0,1},{1,0},{2,3},{3,2},{4,5},{5,4},{6,7},{7,6},{8,9},{9,8},{10,11... | collective-permute-start | bytes 3538952 | tf_op jit(solution)/shard_map/ppermute | solution.py:231
  778.9 58.6 %collective-permute-start.42 = (bf16[1152,384]{1,0:T(8,128)(2,1)S(1)}, bf16[1152,384]{1,0:T(8,128)(2,1)S(1)}, u32[]{:S(2)}, u32[]{:S(2)}) collective-permute-start(bf16[1152,384]{1,0:T(8,128)(2,1)S(1)} %pad_maximum_fusion.4), channel_id=1, source_target_pairs={{0,2},{2,0},{4,6},{6,4},{8,10},{10,8},{12,14},{14,12},{16,18},{18,... | collective-permute-start | bytes 2654216 | tf_op jit(solution)/shard_map/ppermute | solution.py:228
  779.2 59.6 %collective-permute-start.52 = (bf16[1152,384]{1,0:T(8,128)(2,1)S(1)}, bf16[1152,384]{1,0:T(8,128)(2,1)S(1)}, u32[]{:S(2)}, u32[]{:S(2)}) collective-permute-start(bf16[1152,384]{1,0:T(8,128)(2,1)S(1)} %pad_maximum_fusion.5), channel_id=1, source_target_pairs={{0,2},{2,0},{4,6},{6,4},{8,10},{10,8},{12,14},{14,12},{16,18},{18,... | collective-permute-start | bytes 2654216 | tf_op jit(solution)/shard_map/ppermute | solution.py:228
  834.3 27.7 %collective-permute-start.91 = (bf16[768,384]{1,0:T(8,128)(2,1)S(1)}, bf16[768,384]{1,0:T(8,128)(2,1)S(1)}, u32[]{:S(2)}, u32[]{:S(2)}) collective-permute-start(bf16[768,384]{1,0:T(8,128)(2,1)S(1)} %pad_maximum_fusion.7), channel_id=1, source_target_pairs={{0,4},{2,6},{4,0},{6,2},{8,12},{10,14},{12,8},{14,10},{16,20},{18,... | collective-permute-start | bytes 1769480 | tf_op jit(solution)/shard_map/ppermute | solution.py:228
  835.9 38.8 %collective-permute-start.96 = (bf16[192,1536]{1,0:T(8,128)(2,1)S(1)}, bf16[192,1536]{1,0:T(8,128)(2,1)S(1)}, u32[]{:S(2)}, u32[]{:S(2)}) collective-permute-start(bf16[192,1536]{1,0:T(8,128)(2,1)S(1)} %dynamic-slice_convert_fusion.1), channel_id=1, source_target_pairs={{0,4},{2,6},{4,0},{6,2},{8,12},{10,14},{12,8},{14,10},{16,20},{18,... | collective-permute-start | bytes 1769480 | tf_op jit(solution)/shard_map/ppermute | solution.py:228
  837.5 47.1 %collective-permute-start.106 = (bf16[192,1536]{1,0:T(8,128)(2,1)S(1)}, bf16[192,1536]{1,0:T(8,128)(2,1)S(1)}, u32[]{:S(2)}, u32[]{:S(2)}) collective-permute-start(bf16[192,1536]{1,0:T(8,128)(2,1)S(1)} %dynamic-slice_convert_fusion), channel_id=1, source_target_pairs={{0,4},{2,6},{4,0},{6,2},{8,12},{10,14},{12,8},{14,10},{16,20},{18,... | collective-permute-start | bytes 1769480 | tf_op jit(solution)/shard_map/ppermute | solution.py:228
  849.7 78.2 %collective-permute-start.82 = (bf16[1536,384]{1,0:T(8,128)(2,1)S(1)}, bf16[1536,384]{1,0:T(8,128)(2,1)S(1)}, u32[]{:S(2)}, u32[]{:S(2)}) collective-permute-start(bf16[1536,384]{1,0:T(8,128)(2,1)S(1)} %pad_maximum_fusion), channel_id=1, source_target_pairs={{0,2},{2,0},{4,6},{6,4},{8,10},{10,8},{12,14},{14,12},{16,18},{18,... | collective-permute-start | bytes 3538952 | tf_op jit(solution)/shard_map/ppermute | solution.py:228
  862.4 86.5 %collective-permute-start.92 = (bf16[1536,384]{1,0:T(8,128)(2,1)S(1)}, bf16[1536,384]{1,0:T(8,128)(2,1)S(1)}, u32[]{:S(2)}, u32[]{:S(2)}) collective-permute-start(bf16[1536,384]{1,0:T(8,128)(2,1)S(1)} %pad_maximum_fusion.1), channel_id=1, source_target_pairs={{0,2},{2,0},{4,6},{6,4},{8,10},{10,8},{12,14},{14,12},{16,18},{18,... | collective-permute-start | bytes 3538952 | tf_op jit(solution)/shard_map/ppermute | solution.py:228
  (166 other events, 1735.3 us)
